TPU v7x, 32 devices: a whole 2x2x4 slice. The times are simulated.
32 devices in a mesh: ma: 16 (over z, y, core), freq: 2 (over x).
Axes of the slice: x: 2, y: 2, z: 4, core: 2. Of those that a mesh axis runs over, the one named last changes fastest.
Arguments:
- right_side: float32 [128, 8, 2, 512], P('ma', 'freq'), may hold values from -60 to 60
- start_field: float32 [128, 8, 2, 512], P('ma', 'freq'), may hold values from -6 to 6
- beam: float32 [128, 8, 2, 16, 512], P('ma', 'freq'), may hold values from -0.75 to 0.75
- noise: float32 [128, 8, 16], P('ma', 'freq'), may hold values from 0.3 to 3
- inv_power: float32 [512], replicated, may hold values from 0.5 to 2
- smooth: float32 [512], replicated, may hold values from 0.5 to 4
Outputs:
- solution_field: float32 [128, 8, 2, 512], P('ma', 'freq')
- residual: float32 [128, 8, 2, 512], P('ma', 'freq')
All inputs are finite; a program needn't handle non-finite values.
Results may differ from a plain program's by a relative error of at most 0.0003.
Values sent between devices are 32-bit elements; how exact they have to be, the bound alone decides.
A program may use at most 64 MiB of HBM per device.

v0:
```python
import jax
import jax.numpy as jnp
from jax import lax
from jax.sharding import PartitionSpec as P

ITERS = 2


def extended(array, sides, width):
    for axis, dim in sides:
        size, length = (lax.axis_size(axis), array.shape[dim])
        up = [(i, (i + 1) % size) for i in range(size - 1)]
        down = [(j, i) for i, j in up]
        last = lax.slice_in_dim(array, length - width, length, axis=dim)
        leading = lax.slice_in_dim(array, 0, width, axis=dim)
        before = lax.ppermute(last, axis, up)
        after = lax.ppermute(leading, axis, down)
        array = jnp.concatenate([before, array, after], axis=dim)
    return array


def beam_image(field, beam, noise):
    projected = jnp.einsum("mfakl,mfbl->mfabk", beam, field, precision=lax.Precision.HIGHEST)
    real_part = projected[:, :, 0, 0] + projected[:, :, 1, 1]
    imaginary = projected[:, :, 0, 1] - projected[:, :, 1, 0]
    weighted = jnp.stack([real_part, imaginary], axis=2) * noise[:, :, None, :]
    back = jnp.einsum("mfakl,mfbk->mfabl", beam, weighted, precision=lax.Precision.HIGHEST)
    return jnp.stack(
        [back[:, :, 0, 0] - back[:, :, 1, 1], back[:, :, 0, 1] + back[:, :, 1, 0]], axis=2
    )


def prior_term(padded, field, first, total, smooth):
    channel = first + jnp.arange(field.shape[1], dtype=jnp.int32)
    weight = (channel > 0).astype(jnp.float32) + (channel < total - 1).astype(jnp.float32)
    return smooth * (weight[None, :, None, None] * field - padded[:, :-2] - padded[:, 2:])


def two_products(vector, applied):
    return lax.psum((jnp.sum(vector * vector), jnp.sum(vector * applied)), ("ma", "freq"))


def shards(right_side, start_field, beam, noise, inv_power, smooth):
    first = lax.axis_index("freq") * right_side.shape[1]
    total = right_side.shape[1] * lax.axis_size("freq")

    def padded_of(field):
        return extended(field, (("freq", 1),), 1)

    def operate(field):
        prior = prior_term(padded_of(field), field, first, total, smooth)
        return beam_image(field, beam, noise) + inv_power * field + prior

    solution = start_field
    resid_now = right_side - operate(start_field)
    applied = operate(resid_now)
    norm_now, curve_now = two_products(resid_now, applied)
    step_size = norm_now / curve_now
    direction = resid_now
    along = applied
    for turn in range(ITERS):
        solution = solution + step_size * direction
        resid_now = resid_now - step_size * along
        if turn + 1 < ITERS:
            applied = operate(resid_now)
            norm_next, curve_now = two_products(resid_now, applied)
            growth = norm_next / norm_now
            step_size = norm_next / (curve_now - growth * norm_next / step_size)
            direction = resid_now + growth * direction
            along = applied + growth * along
            norm_now = norm_next
    return (solution, resid_now)


def solution(mesh):
    in_specs = (
        P("ma", "freq", None, None),
        P("ma", "freq", None, None),
        P("ma", "freq", None, None, None),
        P("ma", "freq", None),
        P(),
        P(),
    )
    out_specs = (P("ma", "freq", None, None), P("ma", "freq", None, None))
    return jax.shard_map(shards, mesh=mesh, in_specs=in_specs, out_specs=out_specs, check_vma=False)
```

profile of v0, /device:TPU:0, one launch (start us, length us, event | category | flops | bytes accessed | tf_op | source)
XLA Modules:
  0.0 144.0 jit_solution(10948142598104500641)
XLA Ops:
  0.6 0.0 copy-start
  0.6 0.0 copy-start.2
  0.7 0.9 fusion.42
  1.6 4.9 %collective-permute-start = (f32[8,1,2,512]{3,2,1,0:T(2,128)S(1)}, f32[8,1,2,512]{3,2,1,0:T(2,128)S(1)}, u32[]{:S(2)}, u32[]{:S(2)}) collective-permute-start(f32[8,1,2,512]{3,2,1,0:T(2,128)S(1)} %get-tuple-element.22), channel_id=1, source_target_pairs={{0,1},{2,3},{4,5},{6,7},{8,9},{10,11},{12,13},{14,15},{16,17},{18,... | collective-permute-start | bytes 98312 | tf_op jit(solution)/shard_map/ppermute | solution.py:16
  6.5 1.3 collective-permute-start.1
  7.8 0.0 copy-done
  7.8 8.3 %convolution_bitcast_fusion.1 = f32[8,4,2,2,16]{4,3,2,1,0:T(2,128)S(1)} fusion(f32[8,4,2,16,512]{4,3,2,1,0:T(8,128)S(1)} %copy-done, f32[8,4,2,512]{3,2,1,0:T(2,128)} %param.7), kind=kOutput, calls=%fused_computation.1 | convolution fusion | flops 12582912 | bytes 2236416 | tf_op jit(solution)/shard_map/mfakl,mfbl->mfabk/dot_general | solution.py:23
  16.1 0.0 copy-start.1
  16.1 0.0 copy-start.3
  16.1 0.0 copy-start.4
  16.1 0.0 copy-start.5
  16.2 0.0 copy-done.2
  16.2 1.1 convolution_bitcast_fusion
  17.3 0.1 fusion.22
  17.4 0.1 fusion.24
  17.6 0.0 collective-permute-done
  17.6 0.0 collective-permute-done.1
  17.6 0.0 copy-done.1
  17.6 0.0 copy-done.3
  17.6 0.0 copy-done.4
  17.6 0.0 copy-done.5
  17.6 0.3 fusion.11
  17.9 7.4 %fusion.15 = f32[8,4,2,2,16]{4,2,3,1,0:T(2,128)S(1)} fusion(f32[8,4,2,16,512]{4,3,2,1,0:T(8,128)S(1)} %copy-done, f32[8,4,2,512]{3,2,1,0:T(2,128)S(1)} %fusion.11), kind=kOutput, calls=%fused_computation.28 | convolution fusion | flops 12582912 | bytes 2236416 | tf_op jit(solution)/shard_map/mfakl,mfbl->mfabk/dot_general | solution.py:23
  25.4 1.3 fusion.30
  26.7 0.1 copy.46
  26.9 4.5 %collective-permute-start.2 = (f32[8,1,2,512]{3,2,1,0:T(2,128)S(1)}, f32[8,1,2,512]{3,2,1,0:T(2,128)S(1)}, u32[]{:S(2)}, u32[]{:S(2)}) collective-permute-start(f32[8,1,2,512]{3,2,1,0:T(2,128)S(1)} %get-tuple-element.20), channel_id=1, source_target_pairs={{0,1},{2,3},{4,5},{6,7},{8,9},{10,11},{12,13},{14,15},{16,17},{18,... | collective-permute-start | bytes 98312 | tf_op jit(solution)/shard_map/ppermute | solution.py:16
  31.4 1.3 collective-permute-start.3
  32.7 0.1 fusion.21
  32.9 0.1 collective-permute-done.2
  33.0 4.2 %collective-permute-done.3 = f32[8,1,2,512]{3,2,1,0:T(2,128)S(1)} collective-permute-done((f32[8,1,2,512]{3,2,1,0:T(2,128)S(1)}, f32[8,1,2,512]{3,2,1,0:T(2,128)S(1)}, u32[]{:S(2)}, u32[]{:S(2)}) %collective-permute-start.3) | collective-permute-done | bytes 32800 | tf_op jit(solution)/shard_map/ppermute | solution.py:17
  37.2 1.1 multiply_reduce_fusion.2
  38.3 39.8 %all-reduce.1 = (f32[]{:T(128)}, f32[]{:T(128)}) all-reduce(f32[]{:T(128)} %get-tuple-element.5, f32[]{:T(128)} %get-tuple-element.4), channel_id=1, replica_groups=mesh['ma'=16,'freq'=2] {'ma','freq'}, use_global_device_ids=true, to_apply=%region_1.0 | all-reduce | flops 2 | bytes 16 | tf_op jit(solution)/shard_map/psum | solution.py:40
  79.4 7.4 %fusion.13 = f32[8,4,2,2,16]{4,2,3,1,0:T(2,128)S(1)} fusion(f32[8,4,2,16,512]{4,3,2,1,0:T(8,128)S(1)} %copy-done, f32[8,4,2,512]{3,2,1,0:T(2,128)S(1)} %bitcast.90), kind=kOutput, calls=%fused_computation.26 | convolution fusion | flops 12582912 | bytes 2236416 | tf_op jit(solution)/shard_map/mfakl,mfbl->mfabk/dot_general | solution.py:23
  86.9 1.1 fusion.28
  88.0 0.1 copy.45
  88.2 4.2 %collective-permute-start.4 = (f32[8,1,2,512]{3,2,1,0:T(2,128)S(1)}, f32[8,1,2,512]{3,2,1,0:T(2,128)S(1)}, u32[]{:S(2)}, u32[]{:S(2)}) collective-permute-start(f32[8,1,2,512]{3,2,1,0:T(2,128)S(1)} %get-tuple-element.18), channel_id=1, source_target_pairs={{0,1},{2,3},{4,5},{6,7},{8,9},{10,11},{12,13},{14,15},{16,17},{18,... | collective-permute-start | bytes 98312 | tf_op jit(solution)/shard_map/ppermute | solution.py:16
  92.4 1.3 collective-permute-start.5
  93.7 0.1 fusion.19
  93.8 0.1 collective-permute-done.4
  93.9 4.2 %collective-permute-done.5 = f32[8,1,2,512]{3,2,1,0:T(2,128)S(1)} collective-permute-done((f32[8,1,2,512]{3,2,1,0:T(2,128)S(1)}, f32[8,1,2,512]{3,2,1,0:T(2,128)S(1)}, u32[]{:S(2)}, u32[]{:S(2)}) %collective-permute-start.5) | collective-permute-done | bytes 32800 | tf_op jit(solution)/shard_map/ppermute | solution.py:17
  98.2 1.1 multiply_reduce_fusion
  99.3 39.4 %all-reduce = (f32[]{:T(128)}, f32[]{:T(128)}) all-reduce(f32[]{:T(128)} %get-tuple-element.3, f32[]{:T(128)} %get-tuple-element.2), channel_id=1, replica_groups=mesh['ma'=16,'freq'=2] {'ma','freq'}, use_global_device_ids=true, to_apply=%region_5.0 | all-reduce | flops 2 | bytes 16 | tf_op jit(solution)/shard_map/psum | solution.py:40
  143.3 0.8 multiply_subtract_fusion
  (13 shorter events, 0.2 us)
Async XLA Ops:
  0.6 7.1 %copy-start = (f32[8,4,2,16,512]{4,3,2,1,0:T(8,128)S(1)}, f32[8,4,2,16,512]{4,3,2,1,0:T(8,128)}, u32[]{:S(2)}) copy-start(f32[8,4,2,16,512]{4,3,2,1,0:T(8,128)} %param.8) | copy-start | bytes 6291460
  0.6 15.5 %copy-start.2 = (f32[8,4,16]{2,1,0:T(4,128)S(1)}, f32[8,4,16]{2,1,0:T(4,128)}, u32[]{:S(2)}) copy-start(f32[8,4,16]{2,1,0:T(4,128)} %param.9) | copy-start | bytes 6148
  1.6 16.0 %collective-permute-start = (f32[8,1,2,512]{3,2,1,0:T(2,128)S(1)}, f32[8,1,2,512]{3,2,1,0:T(2,128)S(1)}, u32[]{:S(2)}, u32[]{:S(2)}) collective-permute-start(f32[8,1,2,512]{3,2,1,0:T(2,128)S(1)} %get-tuple-element.22), channel_id=1, source_target_pairs={{0,1},{2,3},{4,5},{6,7},{8,9},{10,11},{12,13},{14,15},{16,17},{18,... | collective-permute-start | bytes 98312 | tf_op jit(solution)/shard_map/ppermute | solution.py:16
  6.5 11.1 %collective-permute-start.1 = (f32[8,1,2,512]{3,2,1,0:T(2,128)S(1)}, f32[8,1,2,512]{3,2,1,0:T(2,128)S(1)}, u32[]{:S(2)}, u32[]{:S(2)}) collective-permute-start(f32[8,1,2,512]{3,2,1,0:T(2,128)S(1)} %get-tuple-element.23), channel_id=1, source_target_pairs={{1,0},{3,2},{5,4},{7,6},{9,8},{11,10},{13,12},{15,14},{17,16},{19,... | collective-permute-start | bytes 98312 | tf_op jit(solution)/shard_map/ppermute | solution.py:17
  16.1 1.5 %copy-start.1 = (f32[8,4,2,512]{3,2,1,0:T(2,128)S(1)}, f32[8,4,2,512]{3,2,1,0:T(2,128)}, u32[]{:S(2)}) copy-start(f32[8,4,2,512]{3,2,1,0:T(2,128)} %param.7) | copy-start | bytes 393220
  16.1 1.5 %copy-start.3 = (f32[8,4,2,512]{3,2,1,0:T(2,128)S(1)}, f32[8,4,2,512]{3,2,1,0:T(2,128)}, u32[]{:S(2)}) copy-start(f32[8,4,2,512]{3,2,1,0:T(2,128)} %param.6) | copy-start | bytes 393220
  16.1 1.6 %copy-start.4 = (f32[512]{0:T(512)S(1)}, f32[512]{0:T(512)}, u32[]{:S(2)}) copy-start(f32[512]{0:T(512)} %param.11) | copy-start | bytes 6148
  16.1 1.5 %copy-start.5 = (f32[512]{0:T(512)S(1)}, f32[512]{0:T(512)}, u32[]{:S(2)}) copy-start(f32[512]{0:T(512)} %param.10) | copy-start | bytes 6148
  26.9 6.1 %collective-permute-start.2 = (f32[8,1,2,512]{3,2,1,0:T(2,128)S(1)}, f32[8,1,2,512]{3,2,1,0:T(2,128)S(1)}, u32[]{:S(2)}, u32[]{:S(2)}) collective-permute-start(f32[8,1,2,512]{3,2,1,0:T(2,128)S(1)} %get-tuple-element.20), channel_id=1, source_target_pairs={{0,1},{2,3},{4,5},{6,7},{8,9},{10,11},{12,13},{14,15},{16,17},{18,... | collective-permute-start | bytes 98312 | tf_op jit(solution)/shard_map/ppermute | solution.py:16
  31.4 5.8 %collective-permute-start.3 = (f32[8,1,2,512]{3,2,1,0:T(2,128)S(1)}, f32[8,1,2,512]{3,2,1,0:T(2,128)S(1)}, u32[]{:S(2)}, u32[]{:S(2)}) collective-permute-start(f32[8,1,2,512]{3,2,1,0:T(2,128)S(1)} %get-tuple-element.21), channel_id=1, source_target_pairs={{1,0},{3,2},{5,4},{7,6},{9,8},{11,10},{13,12},{15,14},{17,16},{19,... | collective-permute-start | bytes 98312 | tf_op jit(solution)/shard_map/ppermute | solution.py:17
  88.2 5.8 %collective-permute-start.4 = (f32[8,1,2,512]{3,2,1,0:T(2,128)S(1)}, f32[8,1,2,512]{3,2,1,0:T(2,128)S(1)}, u32[]{:S(2)}, u32[]{:S(2)}) collective-permute-start(f32[8,1,2,512]{3,2,1,0:T(2,128)S(1)} %get-tuple-element.18), channel_id=1, source_target_pairs={{0,1},{2,3},{4,5},{6,7},{8,9},{10,11},{12,13},{14,15},{16,17},{18,... | collective-permute-start | bytes 98312 | tf_op jit(solution)/shard_map/ppermute | solution.py:16
  92.4 5.8 %collective-permute-start.5 = (f32[8,1,2,512]{3,2,1,0:T(2,128)S(1)}, f32[8,1,2,512]{3,2,1,0:T(2,128)S(1)}, u32[]{:S(2)}, u32[]{:S(2)}) collective-permute-start(f32[8,1,2,512]{3,2,1,0:T(2,128)S(1)} %get-tuple-element.19), channel_id=1, source_target_pairs={{1,0},{3,2},{5,4},{7,6},{9,8},{11,10},{13,12},{15,14},{17,16},{19,... | collective-permute-start | bytes 98312 | tf_op jit(solution)/shard_map/ppermute | solution.py:17
where the time goes:
time: 145 us; the launch traced here: 144 us
  blocking collectives  79.2 us (55%)
  matrix products  26.7 us (18%)
  starting transfers between devices  17.5 us (12%)
  waiting for transfers between devices  8.73 us (6%)
  between operations  6.85 us (5%)
  other arithmetic  3.86 us (3%)
    psum x2, blocking collectives, two_products(): lax.psum((jnp.sum(vector * vector), jnp.sum(vector * applied)), ('ma', 'f...  79.2 us
    dot_general x3, matrix products, beam_image(): jnp.einsum('mfakl,mfbl->mfabk', beam, field, precision=lax.Precision.HIGH...  23.1 us
    ppermute x3, starting transfers between devices, extended(): before = lax.ppermute(last, axis, up)  13.6 us
    ppermute x3, waiting for transfers between devices, extended(): after = lax.ppermute(leading, axis, down)  8.46 us
    ppermute x3, starting transfers between devices, extended(): after = lax.ppermute(leading, axis, down)  3.88 us
    dot_general x3, matrix products, beam_image(): jnp.einsum('mfakl,mfbk->mfabl', beam, weighted, precision=lax.Precision.H...  3.6 us
  transfers between devices with their start and end apart: 6, of which 4 were waited for; matrix products, arithmetic and copies ran while one was open for 7% of the time, Pallas kernels for 0%

commit v1 on v0

v1 whole, which is shorter than its diff:
```python
import functools

import jax
import jax.numpy as jnp
from jax import lax
from jax.experimental import pallas as pl
from jax.experimental.pallas import tpu as pltpu
from jax.sharding import PartitionSpec as P

MESH = pl.DeviceIdType.MESH
F32, BF16 = jnp.float32, jnp.bfloat16


def split(x):
    high = x.astype(BF16)
    return high, (x - high.astype(F32)).astype(BF16)


def times(x, high, low, transposed):
    dims = (((1,), (1 if transposed else 0,)), ((), ()))
    rows = x.shape[0]
    x_high, x_low = split(x)
    both = jnp.concatenate([x_high, x_low], axis=0)
    main = lax.dot_general(both, high, dims, preferred_element_type=F32)
    rest = lax.dot_general(x_high, low, dims, preferred_element_type=F32)
    return main[:rows] + (main[rows:] + rest)


def kernel(
    nma, nf, rhs_in, x0_in, beam_in, noise_in, power_in, smooth_in, sol_out, res_out,
    rhs_s, x0_s, beam_s, noise_s, power_s, smooth_s, sol_s, res_s,
    high_s, low_s, x_s, y_s, r_s, u_s, w_s, mask_s, halo_s, message_s, all_s,
    in_sem, beam_sem, out_sem, halo_send, halo_recv, sum_send, sum_recv,
):
    modes, freqs, _, ell = rhs_in.shape
    rank = beam_in.shape[3]
    width = modes * rank
    n = nma * nf
    my_ma, my_f = lax.axis_index("ma"), lax.axis_index("freq")
    me = my_ma * nf + my_f
    last = freqs - 1
    order = [last] + ([0] if last else []) + list(range(1, last))

    x0_copy = pltpu.make_async_copy(x0_in, x0_s, in_sem.at[0])
    small = [
        pltpu.make_async_copy(power_in, power_s, in_sem.at[1]),
        pltpu.make_async_copy(smooth_in, smooth_s, in_sem.at[2]),
        pltpu.make_async_copy(noise_in, noise_s, in_sem.at[3]),
    ]
    rhs_copy = pltpu.make_async_copy(rhs_in, rhs_s, in_sem.at[4])
    x0_copy.start()
    for copy in small:
        copy.start()
    beam_copies = {}
    for i, f in enumerate(order):
        beam_copies[f] = [
            pltpu.make_async_copy(beam_in.at[:, f, a], beam_s.at[f, a], beam_sem.at[2 * f + a])
            for a in range(2)
        ]
        for copy in beam_copies[f]:
            copy.start()
        if i == 0:
            rhs_copy.start()

    def target(offset):
        ma = my_ma + offset // nf
        other = my_f + offset % nf
        return lax.rem(ma, nma), lax.rem(other, nf)

    barrier = pltpu.get_barrier_semaphore()

    def greet(offset, carry):
        pl.semaphore_signal(barrier, inc=1, device_id=target(offset), device_id_type=MESH)
        return carry

    if n > 64:
        lax.fori_loop(1, n, greet, 0)
    else:
        for offset in range(1, n):
            greet(offset, 0)

    has_left, has_right = my_f > 0, my_f < nf - 1

    def halo_copies(kind, source):
        to_right = pltpu.make_async_remote_copy(
            src_ref=source.at[last], dst_ref=halo_s.at[kind, 0],
            send_sem=halo_send.at[kind, 1], recv_sem=halo_recv.at[kind, 0],
            device_id=(my_ma, my_f + 1), device_id_type=MESH,
        )
        to_left = pltpu.make_async_remote_copy(
            src_ref=source.at[0], dst_ref=halo_s.at[kind, 1],
            send_sem=halo_send.at[kind, 0], recv_sem=halo_recv.at[kind, 1],
            device_id=(my_ma, my_f - 1), device_id_type=MESH,
        )
        return to_right, to_left

    def send(kind, source):
        to_right, to_left = halo_copies(kind, source)
        if nf > 1:
            pl.when(has_right)(to_right.start)
            pl.when(has_left)(to_left.start)

    def arrive(kind, source):
        to_right, to_left = halo_copies(kind, source)
        if nf > 1:
            pl.when(has_left)(to_right.wait_recv)
            pl.when(has_right)(to_left.wait_recv)

    def sent(kind, source):
        to_right, to_left = halo_copies(kind, source)
        if nf > 1:
            pl.when(has_right)(to_right.wait_send)
            pl.when(has_left)(to_left.wait_send)

    @pl.when(jnp.logical_not(has_left))
    def _():
        halo_s[:, 0] = jnp.zeros_like(halo_s[:, 0])

    @pl.when(jnp.logical_not(has_right))
    def _():
        halo_s[:, 1] = jnp.zeros_like(halo_s[:, 1])

    x0_copy.wait()
    for f in range(freqs):
        for b in range(2):
            x_s[f, b * modes:(b + 1) * modes, :] = x0_s[:, f, b, :]
    for copy in small:
        copy.wait()
    pl.semaphore_wait(barrier, n - 1)
    send(0, x_s)

    power, smooth = power_s[...], smooth_s[...]
    own = (
        lax.broadcasted_iota(jnp.int32, (modes, width), 1) // rank
        == lax.broadcasted_iota(jnp.int32, (modes, width), 0)
    )
    for f in range(freqs):
        mask_s[f] = jnp.where(own, jnp.concatenate([noise_s[:, f, :]] * modes, axis=1), 0.0)

    def project(f, field):
        seen = times(field, high_s[f], low_s[f], True)
        real = seen[:modes, :width] + seen[modes:, width:]
        imaginary = seen[modes:, :width] - seen[:modes, width:]
        return real, imaginary, mask_s[f] * real, mask_s[f] * imaginary

    def back(f, real, imaginary):
        weighted = jnp.concatenate(
            [
                jnp.concatenate([real, -imaginary], axis=1),
                jnp.concatenate([imaginary, real], axis=1),
            ],
            axis=0,
        )
        return times(weighted, high_s[f], low_s[f], False)

    def count(f):
        below = jnp.where(has_left, 1.0, 0.0) if f == 0 else 1.0
        above = jnp.where(has_right, 1.0, 0.0) if f == last else 1.0
        return below + above

    def local_prior(f, ref):
        value = count(f) * ref[f]
        if f > 0:
            value = value - ref[f - 1]
        if f < last:
            value = value - ref[f + 1]
        return power * ref[f] + smooth * value

    def apply_beam(f, field):
        _, _, real, imaginary = project(f, field)
        return back(f, real, imaginary)

    for f in order:
        for copy in beam_copies[f]:
            copy.wait()
        high, low = split(beam_s[f].reshape(2 * width, ell))
        high_s[f] = high
        low_s[f] = low
        if f == order[0]:
            rhs_copy.wait()
        rhs = jnp.concatenate([rhs_s[:, f, 0, :], rhs_s[:, f, 1, :]], axis=0)
        y_s[f] = rhs - apply_beam(f, x_s[f]) - local_prior(f, x_s)
        if f == 0:
            send(1, y_s)
    inner = list(range(1, last))
    outer = [f for f in order if f not in inner]
    for f in inner:
        r_s[f] = y_s[f]
    for f in inner:
        u_s[f] = apply_beam(f, r_s[f])
    arrive(0, x_s)
    arrive(1, y_s)
    for f in outer:
        value = y_s[f]
        if f == 0:
            value = value + smooth * halo_s[0, 0]
        if f == last:
            value = value + smooth * halo_s[0, 1]
        r_s[f] = value
    before = jnp.where(has_left, halo_s[1, 0] + smooth * x_s[0], 0.0)
    after = jnp.where(has_right, halo_s[1, 1] + smooth * x_s[last], 0.0)
    for f in outer:
        value = apply_beam(f, r_s[f]) + local_prior(f, r_s)
        if f == 0:
            value = value - smooth * before
        if f == last:
            value = value - smooth * after
        u_s[f] = value
    send(2, u_s)
    for f in inner:
        u_s[f] = u_s[f] + local_prior(f, r_s)
    norm = jnp.zeros((2 * modes, ell), F32)
    curve, square, cube = norm, norm, norm
    beam_part = jnp.zeros((modes, width), F32)
    pending = {}
    for f in inner + outer:
        real, imaginary, real_weighted, imaginary_weighted = project(f, u_s[f])
        pending[f] = real_weighted, imaginary_weighted
        beam_part = beam_part + (real * real_weighted + imaginary * imaginary_weighted)
        w_s[f] = local_prior(f, u_s)
        norm = norm + r_s[f] * r_s[f]
        curve = curve + r_s[f] * u_s[f]
        square = square + u_s[f] * u_s[f]
        cube = cube + u_s[f] * w_s[f]
    arrive(2, u_s)
    before, after = smooth * halo_s[2, 0], smooth * halo_s[2, 1]
    cube = cube - (before * u_s[0] + after * u_s[last])
    lane = lax.broadcasted_iota(jnp.int32, (1, 128), 1)
    message = jnp.zeros((1, 128), F32)
    for i, part in enumerate((norm, curve, square, cube)):
        total = jnp.sum(part, keepdims=True)
        if i == 3:
            total = total + jnp.sum(beam_part, keepdims=True)
        message = jnp.where(lane == i, total, message)
    message_s[0] = message
    all_s[me] = message

    def share(offset, carry):
        pltpu.make_async_remote_copy(
            src_ref=message_s.at[0], dst_ref=all_s.at[me], send_sem=sum_send, recv_sem=sum_recv,
            device_id=target(offset), device_id_type=MESH,
        ).start()
        return carry

    if n > 64:
        lax.fori_loop(1, n, share, 0)
    else:
        for offset in range(1, n):
            share(offset, 0)

    w_s[0] = w_s[0] - before
    w_s[last] = w_s[last] - after
    for f in range(freqs):
        w_s[f] = w_s[f] + back(f, *pending[f])
    for kind, source in enumerate((x_s, y_s, u_s)):
        sent(kind, source)
    if n > 1:
        everything = all_s.at[pl.ds(0, n - 1)]
        pltpu.make_async_copy(everything, everything, sum_recv).wait()
    total = jnp.sum(all_s[...], axis=0)
    m0, m1, m2, m3 = (total[:, i:i + 1] for i in range(4))
    step = m0 / m1
    norm_next = step * (step * m2 - m1)
    curve_next = m1 - 2.0 * step * m2 + step * step * m3
    growth = norm_next / m0
    step_next = norm_next / (curve_next - growth * norm_next / step)
    c = step + step_next * (1.0 + growth)
    e = step * step_next
    for f in range(freqs):
        solved = x_s[f] + c * r_s[f] - e * u_s[f]
        left = r_s[f] - c * u_s[f] + e * w_s[f]
        for b in range(2):
            sol_s[:, f, b, :] = solved[b * modes:(b + 1) * modes]
            res_s[:, f, b, :] = left[b * modes:(b + 1) * modes]
    outs = [
        pltpu.make_async_copy(sol_s, sol_out, out_sem.at[0]),
        pltpu.make_async_copy(res_s, res_out, out_sem.at[1]),
    ]
    for copy in outs:
        copy.start()
    if n > 1:
        everything = all_s.at[pl.ds(0, n - 1)]
        pltpu.make_async_copy(everything, everything, sum_send).wait()
    for copy in outs:
        copy.wait()


def shards(right_side, start_field, beam, noise, inv_power, smooth):
    nma, nf = lax.axis_size("ma"), lax.axis_size("freq")
    modes, freqs, _, ell = right_side.shape
    rank = beam.shape[3]
    width = modes * rank
    any_spec = pl.BlockSpec(memory_space=pl.ANY)
    field = pltpu.VMEM(right_side.shape, F32)
    slab = pltpu.VMEM((freqs, 2 * modes, ell), F32)
    half = pltpu.VMEM((freqs, 2 * width, ell), BF16)
    return pl.pallas_call(
        functools.partial(kernel, nma, nf),
        out_shape=[jax.ShapeDtypeStruct(right_side.shape, F32)] * 2,
        in_specs=[any_spec] * 6,
        out_specs=[any_spec] * 2,
        scratch_shapes=[
            field, field,
            pltpu.VMEM((freqs, 2, modes, rank, ell), F32),
            pltpu.VMEM(noise.shape, F32),
            pltpu.VMEM((1, ell), F32), pltpu.VMEM((1, ell), F32),
            field, field,
            half, half,
            slab, slab, slab, slab, slab,
            pltpu.VMEM((freqs, modes, width), F32),
            pltpu.VMEM((3, 2, 2 * modes, ell), F32),
            pltpu.VMEM((1, 1, 128), F32),
            pltpu.VMEM((nma * nf, 1, 128), F32),
            pltpu.SemaphoreType.DMA((5,)),
            pltpu.SemaphoreType.DMA((2 * freqs,)),
            pltpu.SemaphoreType.DMA((2,)),
            pltpu.SemaphoreType.DMA((3, 2)),
            pltpu.SemaphoreType.DMA((3, 2)),
            pltpu.SemaphoreType.DMA,
            pltpu.SemaphoreType.DMA,
        ],
        compiler_params=pltpu.CompilerParams(collective_id=0, has_side_effects=True),
        name="solve",
    )(right_side, start_field, beam, noise, inv_power[None], smooth[None])


def solution(mesh):
    in_specs = (
        P("ma", "freq", None, None),
        P("ma", "freq", None, None),
        P("ma", "freq", None, None, None),
        P("ma", "freq", None),
        P(),
        P(),
    )
    out_specs = (P("ma", "freq", None, None), P("ma", "freq", None, None))
    return jax.shard_map(shards, mesh=mesh, in_specs=in_specs, out_specs=out_specs, check_vma=False)
```

time: 145 us -> 23.6 us (0.16)
  blocking collectives: 79.2 us -> 0 us
  matrix products: 26.7 us -> 0 us
  Pallas kernels: 0 us -> 19.7 us
  starting transfers between devices: 17.5 us -> 0 us
  waiting for transfers between devices: 8.73 us -> 0 us
  between operations: 6.85 us -> 0.64 us
  other arithmetic: 3.86 us -> 0 us
  local copies, waits for them, and re-layouts: 1.29 us -> 3.14 us
    psum x2 -> x0, blocking collectives: 79.2 us -> none  [two_products(): lax.psum((jnp.sum(vector * vector), jnp.sum(vector * applied)), ('ma', 'f...]
    dot_general x6 -> x0, matrix products: 26.7 us -> none  [the longest x3 23.1 us: beam_image(): jnp.einsum('mfakl,mfbl->mfabk', beam, field, precision=lax.Precision.HIGH...]
    pallas_call x0 -> x1, Pallas kernels: none -> 19.7 us  [shards(): pl.pallas_call(functools.partial(kernel, nma, nf), out_shape=[jax.ShapeDt...]
    ppermute x6 -> x0, starting transfers between devices: 17.5 us -> none  [the longest x3 13.6 us: extended(): before = lax.ppermute(last, axis, up)]
    ppermute x6 -> x0, waiting for transfers between devices: 8.73 us -> none  [the longest x3 8.46 us: extended(): after = lax.ppermute(leading, axis, down)]
    unnamed x12 -> x2, local copies, waits for them, and re-layouts: 0.04 us -> 3.14 us
    reduce_sum x2 -> x0, other arithmetic: 2.2 us -> none  [two_products(): jnp.sum(vector * applied)]
  transfers between devices with their start and end apart: 6 -> 0, of which waited for: 4 -> 0; matrix products, arithmetic and copies ran while one was open for 7% -> 0% of each run, Pallas kernels for 0% -> 0%
where the time goes in v1:
time: 23.6 us; the launch traced here: 23.5 us
  Pallas kernels  19.7 us (83%)
  local copies, waits for them, and re-layouts  3.14 us (13%)
  between operations  0.64 us (3%)
    pallas_call x1, Pallas kernels, shards(): pl.pallas_call(functools.partial(kernel, nma, nf), out_shape=[jax.ShapeDt...  19.7 us
    unnamed x2, local copies, waits for them, and re-layouts  3.14 us

profile of v1, /device:TPU:0, one launch (start us, length us, event | category | flops | bytes accessed | tf_op | source)
XLA Modules:
  0.0 23.5 jit_solution(11327681687731897156)
XLA Ops:
  0.6 19.7 %solve.1 = (f32[8,4,2,512]{3,2,1,0:T(2,128)}, f32[8,4,2,512]{3,2,1,0:T(2,128)}) custom-call(f32[8,4,2,512]{3,2,1,0:T(2,128)} %rhs_in.1, f32[8,4,2,512]{3,2,1,0:T(2,128)} %x0_in.1, f32[8,4,2,16,512]{4,3,2,1,0:T(8,128)} %beam_in.1, f32[8,4,16]{2,1,0:T(4,128)} %noise_in.1, f32[1,512]{1,0:T(1,128)} %bitcast.2, f32[1,512]{1,0:T(1,128)} %bitcast.3), custom_call_target="tpu_custom_call" | custom-call | tf_op jit(solution)/shard_map/solve/pallas_call | solution.py:297
  20.3 1.6 %copy.10 = f32[8,4,2,512]{3,2,1,0:T(2,128)} copy(f32[8,4,2,512]{3,2,1,0:T(2,128)} %get-tuple-element.4) | data formatting | bytes 262144
  21.9 1.6 %copy.11 = f32[8,4,2,512]{3,2,1,0:T(2,128)} copy(f32[8,4,2,512]{3,2,1,0:T(2,128)} %get-tuple-element.5) | data formatting | bytes 262144

commit v2 on v1

v2 whole, which is shorter than its diff:
```python
import functools

import jax
import jax.numpy as jnp
from jax import lax
from jax.experimental import pallas as pl
from jax.experimental.pallas import tpu as pltpu
from jax.sharding import PartitionSpec as P

MESH = pl.DeviceIdType.MESH
F32, BF16 = jnp.float32, jnp.bfloat16


def split(x):
    high = x.astype(BF16)
    return high, (x - high.astype(F32)).astype(BF16)


def times(x, high, low, transposed):
    dims = (((1,), (1 if transposed else 0,)), ((), ()))
    rows = x.shape[0]
    x_high, x_low = split(x)
    both = jnp.concatenate([x_high, x_low], axis=0)
    main = lax.dot_general(both, high, dims, preferred_element_type=F32)
    rest = lax.dot_general(x_high, low, dims, preferred_element_type=F32)
    return main[:rows] + (main[rows:] + rest)


def kernel(
    nma, nf, rhs_in, x0_in, beam_in, noise_in, power_in, smooth_in, sol_s, res_s,
    rhs_s, x0_s, beam_s, noise_s, power_s, smooth_s,
    high_s, low_s, x_s, y_s, r_s, u_s, w_s, mask_s, halo_s, message_s, all_s,
    in_sem, beam_sem, halo_send, halo_recv, sum_send, sum_recv, word_sem,
):
    modes, freqs, _, ell = rhs_in.shape
    rank = beam_in.shape[3]
    width = modes * rank
    n = nma * nf
    my_ma, my_f = lax.axis_index("ma"), lax.axis_index("freq")
    me = my_ma * nf + my_f
    last = freqs - 1
    two_sided = nf > 2

    def at(g):
        return jnp.where(my_f == 0, last - g, g)


    x0_copy = pltpu.make_async_copy(x0_in, x0_s, in_sem.at[0])
    small = [
        pltpu.make_async_copy(power_in, power_s, in_sem.at[1]),
        pltpu.make_async_copy(smooth_in, smooth_s, in_sem.at[2]),
        pltpu.make_async_copy(noise_in, noise_s, in_sem.at[3]),
    ]
    rhs_copy = pltpu.make_async_copy(rhs_in, rhs_s, in_sem.at[4])
    x0_copy.start()
    for copy in small:
        copy.start()
    beam_copies = {}
    for f in range(freqs):
        beam_copies[f] = [
            pltpu.make_async_copy(beam_in.at[:, at(f), a], beam_s.at[f, a], beam_sem.at[2 * f + a])
            for a in range(2)
        ]
        for copy in beam_copies[f]:
            copy.start()
        if f == 0:
            rhs_copy.start()

    def target(offset):
        ma = my_ma + offset // nf
        other = my_f + offset % nf
        return lax.rem(ma, nma), lax.rem(other, nf)

    def partners(size, place):
        distances = [1 << bit for bit in range(size.bit_length() - 1)]
        return [place + d * (1 - 2 * (place // d % 2)) for d in distances]

    word = [(my_ma, other) for other in partners(nf, my_f)]
    word += [(other, my_f) for other in partners(nma, my_ma)]
    barrier = pltpu.get_barrier_semaphore()
    near = jnp.where(my_f == 0, 1, my_f - 1)
    has_far = (my_f > 0) & (my_f < nf - 1)

    def greet(device):
        pl.semaphore_signal(barrier, inc=1, device_id=device, device_id_type=MESH)

    for device in word:
        greet(device)
    expected = len(word)
    if nf > 2:
        pl.when(my_f > 0)(lambda: greet((my_ma, my_f - 1)))
        pl.when(my_f < nf - 1)(lambda: greet((my_ma, my_f + 1)))
        expected = expected + jnp.minimum(my_f, 1) + jnp.minimum(nf - 1 - my_f, 1)

    def pass_word(step):
        if step > 0:
            pl.semaphore_wait(word_sem.at[step - 1], 1)
        if step < len(word):
            pl.semaphore_signal(
                word_sem.at[step], inc=1, device_id=word[step], device_id_type=MESH
            )

    def near_copy(kind, source):
        side = jnp.minimum(my_f // 2, 1) if two_sided else 0
        return pltpu.make_async_remote_copy(
            src_ref=source.at[0], dst_ref=halo_s.at[kind, side],
            send_sem=halo_send.at[kind, 0], recv_sem=halo_recv.at[kind, side],
            device_id=(my_ma, near), device_id_type=MESH,
        )

    def far_copy(kind, source):
        return pltpu.make_async_remote_copy(
            src_ref=source.at[last], dst_ref=halo_s.at[kind, 0],
            send_sem=halo_send.at[kind, 1], recv_sem=halo_recv.at[kind, 0],
            device_id=(my_ma, my_f + 1), device_id_type=MESH,
        )

    def arrival(kind, side):
        slot = halo_s.at[kind, side]
        return pltpu.make_async_copy(slot, slot, halo_recv.at[kind, side])

    def send(kind, source):
        if nf > 1:
            near_copy(kind, source).start()
        if two_sided:
            pl.when(has_far)(lambda: far_copy(kind, source).start())

    def arrive(kind):
        if nf > 1:
            arrival(kind, 0).wait()
        if two_sided:
            pl.when(has_far)(lambda: arrival(kind, 1).wait())

    def sent(kind, source):
        if nf > 1:
            near_copy(kind, source).wait_send()
        if two_sided:
            pl.when(has_far)(lambda: far_copy(kind, source).wait_send())

    if nf == 1:
        halo_s[...] = jnp.zeros_like(halo_s)
    if two_sided:
        @pl.when(jnp.logical_not(has_far))
        def _():
            halo_s[:, 1] = jnp.zeros_like(halo_s[:, 1])

    x0_copy.wait()
    for f in range(freqs):
        for b in range(2):
            x_s[f, b * modes:(b + 1) * modes, :] = x0_s[:, at(f), b, :]
    for copy in small:
        copy.wait()
    pl.semaphore_wait(barrier, expected)
    send(0, x_s)
    pass_word(0)

    power, smooth = power_s[...], smooth_s[...]
    own = (
        lax.broadcasted_iota(jnp.int32, (modes, width), 1) // rank
        == lax.broadcasted_iota(jnp.int32, (modes, width), 0)
    )
    for f in range(freqs):
        mask_s[f] = jnp.where(own, jnp.concatenate([noise_s[:, at(f), :]] * modes, axis=1), 0.0)

    def project(f, field):
        seen = times(field, high_s[f], low_s[f], True)
        real = seen[:modes, :width] + seen[modes:, width:]
        imaginary = seen[modes:, :width] - seen[:modes, width:]
        return real, imaginary, mask_s[f] * real, mask_s[f] * imaginary

    def back(f, real, imaginary):
        weighted = jnp.concatenate(
            [
                jnp.concatenate([real, -imaginary], axis=1),
                jnp.concatenate([imaginary, real], axis=1),
            ],
            axis=0,
        )
        return times(weighted, high_s[f], low_s[f], False)

    def count(f):
        value = float(f > 0) + float(f < last) + float(nf > 1 and f == 0)
        if two_sided and f == last:
            value = value + jnp.where(has_far, 1.0, 0.0)
        return value

    def local_prior(f, ref):
        value = count(f) * ref[f]
        if f > 0:
            value = value - ref[f - 1]
        if f < last:
            value = value - ref[f + 1]
        return power * ref[f] + smooth * value

    def apply_beam(f, field):
        _, _, real, imaginary = project(f, field)
        return back(f, real, imaginary)

    edges = [0, last] if two_sided and last else [0]
    inner = [f for f in range(freqs) if f not in edges]
    for f in edges + inner:
        for copy in beam_copies[f]:
            copy.wait()
        high, low = split(beam_s[f].reshape(2 * width, ell))
        high_s[f] = high
        low_s[f] = low
        if f == 0:
            rhs_copy.wait()
        rhs = jnp.concatenate([rhs_s[:, at(f), 0, :], rhs_s[:, at(f), 1, :]], axis=0)
        y_s[f] = rhs - apply_beam(f, x_s[f]) - local_prior(f, x_s)
        if f == edges[-1]:
            send(1, y_s)
    pass_word(1)
    for f in inner:
        r_s[f] = y_s[f]
        u_s[f] = apply_beam(f, r_s[f])
    pass_word(2)
    arrive(0)
    arrive(1)
    before = after = 0.0
    r_s[0] = y_s[0] + smooth * halo_s[0, 0]
    if nf > 1:
        before = halo_s[1, 0] + smooth * x_s[0]
    if two_sided:
        base = r_s if last == 0 else y_s
        r_s[last] = base[last] + smooth * halo_s[0, 1]
        after = jnp.where(has_far, halo_s[1, 1] + smooth * x_s[last], 0.0)
    for f in edges:
        value = apply_beam(f, r_s[f]) + local_prior(f, r_s)
        if f == 0:
            value = value - smooth * before
        if f == last:
            value = value - smooth * after
        u_s[f] = value
    send(2, u_s)
    passed = 3
    for f in inner:
        u_s[f] = u_s[f] + local_prior(f, r_s)
    norm = jnp.zeros((2 * modes, ell), F32)
    curve, square, cube = norm, norm, norm
    beam_part = jnp.zeros((modes, width), F32)
    pending = {}
    for f in inner + edges:
        real, imaginary, real_weighted, imaginary_weighted = project(f, u_s[f])
        pending[f] = real_weighted, imaginary_weighted
        beam_part = beam_part + (real * real_weighted + imaginary * imaginary_weighted)
        w_s[f] = local_prior(f, u_s)
        norm = norm + r_s[f] * r_s[f]
        curve = curve + r_s[f] * u_s[f]
        square = square + u_s[f] * u_s[f]
        cube = cube + u_s[f] * w_s[f]
    arrive(2)
    before = smooth * halo_s[2, 0]
    cube = cube - before * u_s[0]
    if two_sided:
        after = smooth * halo_s[2, 1]
        cube = cube - after * u_s[last]
    lane = lax.broadcasted_iota(jnp.int32, (1, 128), 1)
    message = jnp.zeros((1, 128), F32)
    for i, part in enumerate((norm, curve, square, cube)):
        total = jnp.sum(part, keepdims=True)
        if i == 3:
            total = total + jnp.sum(beam_part, keepdims=True)
        message = jnp.where(lane == i, total, message)
    message_s[0] = message
    all_s[me] = message

    for step in range(passed, len(word) + 1):
        pass_word(step)

    def share(offset, carry):
        pltpu.make_async_remote_copy(
            src_ref=message_s.at[0], dst_ref=all_s.at[me], send_sem=sum_send, recv_sem=sum_recv,
            device_id=target(offset), device_id_type=MESH,
        ).start()
        return carry

    if n > 64:
        lax.fori_loop(1, n, share, 0)
    else:
        for offset in range(1, n):
            share(offset, 0)

    w_s[0] = w_s[0] - before
    if two_sided:
        w_s[last] = w_s[last] - after
    for f in range(freqs):
        w_s[f] = w_s[f] + back(f, *pending[f])
    for kind, source in enumerate((x_s, y_s, u_s)):
        sent(kind, source)
    if n > 1:
        everything = all_s.at[pl.ds(0, n - 1)]
        pltpu.make_async_copy(everything, everything, sum_recv).wait()
    total = jnp.sum(all_s[...], axis=0)
    m0, m1, m2, m3 = (total[:, i:i + 1] for i in range(4))
    step = m0 / m1
    norm_next = step * (step * m2 - m1)
    curve_next = m1 - 2.0 * step * m2 + step * step * m3
    growth = norm_next / m0
    step_next = norm_next / (curve_next - growth * norm_next / step)
    c = step + step_next * (1.0 + growth)
    e = step * step_next
    for f in range(freqs):
        solved = x_s[f] + c * r_s[f] - e * u_s[f]
        left = r_s[f] - c * u_s[f] + e * w_s[f]
        for b in range(2):
            sol_s[:, at(f), b, :] = solved[b * modes:(b + 1) * modes]
            res_s[:, at(f), b, :] = left[b * modes:(b + 1) * modes]
    if n > 1:
        everything = all_s.at[pl.ds(0, n - 1)]
        pltpu.make_async_copy(everything, everything, sum_send).wait()


def write_out(sol_in, res_in, sol_out, res_out, sem):
    copies = [
        pltpu.make_async_copy(sol_in, sol_out, sem.at[0]),
        pltpu.make_async_copy(res_in, res_out, sem.at[1]),
    ]
    for copy in copies:
        copy.start()
    for copy in copies:
        copy.wait()


def shards(right_side, start_field, beam, noise, inv_power, smooth):
    nma, nf = lax.axis_size("ma"), lax.axis_size("freq")
    modes, freqs, _, ell = right_side.shape
    rank = beam.shape[3]
    width = modes * rank
    vmem_spec = pl.BlockSpec(memory_space=pltpu.VMEM)
    any_spec = pl.BlockSpec(memory_space=pl.ANY)
    field = pltpu.VMEM(right_side.shape, F32)
    slab = pltpu.VMEM((freqs, 2 * modes, ell), F32)
    half = pltpu.VMEM((freqs, 2 * width, ell), BF16)
    outs = pl.pallas_call(
        functools.partial(kernel, nma, nf),
        out_shape=[field] * 2,
        in_specs=[any_spec] * 6,
        out_specs=[vmem_spec] * 2,
        scratch_shapes=[
            field, field,
            pltpu.VMEM((freqs, 2, modes, rank, ell), F32),
            pltpu.VMEM(noise.shape, F32),
            pltpu.VMEM((1, ell), F32), pltpu.VMEM((1, ell), F32),
            half, half,
            slab, slab, slab, slab, slab,
            pltpu.VMEM((freqs, modes, width), F32),
            pltpu.VMEM((3, 2, 2 * modes, ell), F32),
            pltpu.VMEM((1, 1, 128), F32),
            pltpu.VMEM((nma * nf, 1, 128), F32),
            pltpu.SemaphoreType.DMA((5,)),
            pltpu.SemaphoreType.DMA((2 * freqs,)),
            pltpu.SemaphoreType.DMA((3, 2)),
            pltpu.SemaphoreType.DMA((3, 2)),
            pltpu.SemaphoreType.DMA,
            pltpu.SemaphoreType.DMA,
            pltpu.SemaphoreType.REGULAR(((nma * nf).bit_length(),)),
        ],
        compiler_params=pltpu.CompilerParams(
            collective_id=0, has_side_effects=True, vmem_limit_bytes=67043328 - 2 * right_side.size * 4
        ),
        name="solve",
    )(right_side, start_field, beam, noise, inv_power[None], smooth[None])
    return pl.pallas_call(
        write_out,
        out_shape=[jax.ShapeDtypeStruct(right_side.shape, F32)] * 2,
        in_specs=[vmem_spec] * 2,
        out_specs=[any_spec] * 2,
        scratch_shapes=[pltpu.SemaphoreType.DMA((2,))],
        compiler_params=pltpu.CompilerParams(vmem_limit_bytes=1024 * 1024),
        name="write_out",
    )(*outs)


def solution(mesh):
    in_specs = (
        P("ma", "freq", None, None),
        P("ma", "freq", None, None),
        P("ma", "freq", None, None, None),
        P("ma", "freq", None),
        P(),
        P(),
    )
    out_specs = (P("ma", "freq", None, None), P("ma", "freq", None, None))
    return jax.shard_map(shards, mesh=mesh, in_specs=in_specs, out_specs=out_specs, check_vma=False)
```

time: 23.6 us -> 22 us (0.932)
  local copies, waits for them, and re-layouts: 3.14 us -> 0 us
  Pallas kernels: 19.7 us -> 21.2 us
    unnamed x2 -> x0, local copies, waits for them, and re-layouts: 3.14 us -> none
    pallas_call x1 -> x2, Pallas kernels: 19.7 us -> 21.2 us  [the longest x1 20.5 us: shards(): pl.pallas_call(functools.partial(kernel, nma, nf), out_shape=[field] * 2,...]
where the time goes in v2:
time: 22 us; the launch traced here: 21.8 us
  Pallas kernels  21.2 us (96%)
  between operations  0.64 us (3%)
    pallas_call x1, Pallas kernels, shards(): pl.pallas_call(functools.partial(kernel, nma, nf), out_shape=[field] * 2,...  20.5 us
    pallas_call x1, Pallas kernels, shards(): pl.pallas_call(write_out, out_shape=[jax.ShapeDtypeStruct(right_side.shap...  0.72 us

profile of v2, /device:TPU:0, one launch (start us, length us, event | category | flops | bytes accessed | tf_op | source)
XLA Modules:
  0.0 21.8 jit_solution(4757916706210116120)
XLA Ops:
  0.6 20.5 %solve.1 = (f32[8,4,2,512]{3,2,1,0:T(2,128)S(1)}, f32[8,4,2,512]{3,2,1,0:T(2,128)S(1)}) custom-call(f32[8,4,2,512]{3,2,1,0:T(2,128)} %rhs_in.1, f32[8,4,2,512]{3,2,1,0:T(2,128)} %x0_in.1, f32[8,4,2,16,512]{4,3,2,1,0:T(8,128)} %beam_in.1, f32[8,4,16]{2,1,0:T(4,128)} %noise_in.1, f32[1,512]{1,0:T(1,128)} %bitcast.2, f32[1,512]{1,0:T(1,128)} %bitcast.3), custom_call_target="tpu_custom_call" | custom-call | tf_op jit(solution)/shard_map/solve/pallas_call | solution.py:335
  21.1 0.7 %write_out.1 = (f32[8,4,2,512]{3,2,1,0:T(2,128)}, f32[8,4,2,512]{3,2,1,0:T(2,128)}) custom-call(f32[8,4,2,512]{3,2,1,0:T(2,128)S(1)} %get-tuple-element.4.sol_in, f32[8,4,2,512]{3,2,1,0:T(2,128)S(1)} %get-tuple-element.5.res_in), custom_call_target="tpu_custom_call" | custom-call | tf_op jit(solution)/shard_map/write_out/pallas_call | solution.py:364

commit v3 on v2

--- a/solution.py
+++ b/solution.py
@@ -196,6 +196,12 @@
         _, _, real, imaginary = project(f, field)
         return back(f, real, imaginary)
 
+    steps = list(range(1, len(word) + 1))
+
+    def advance():
+        if steps:
+            pass_word(steps.pop(0))
+
     edges = [0, last] if two_sided and last else [0]
     inner = [f for f in range(freqs) if f not in edges]
     for f in edges + inner:
@@ -210,11 +216,12 @@
         y_s[f] = rhs - apply_beam(f, x_s[f]) - local_prior(f, x_s)
         if f == edges[-1]:
             send(1, y_s)
-    pass_word(1)
+        elif f in inner:
+            advance()
     for f in inner:
         r_s[f] = y_s[f]
         u_s[f] = apply_beam(f, r_s[f])
-    pass_word(2)
+        advance()
     arrive(0)
     arrive(1)
     before = after = 0.0
@@ -233,7 +240,6 @@
             value = value - smooth * after
         u_s[f] = value
     send(2, u_s)
-    passed = 3
     for f in inner:
         u_s[f] = u_s[f] + local_prior(f, r_s)
     norm = jnp.zeros((2 * modes, ell), F32)
@@ -265,8 +271,8 @@
     message_s[0] = message
     all_s[me] = message
 
-    for step in range(passed, len(word) + 1):
-        pass_word(step)
+    while steps:
+        advance()
 
     def share(offset, carry):
         pltpu.make_async_remote_copy(

time: 22 us -> 20.9 us (0.950)
  Pallas kernels: 21.2 us -> 20.1 us
    pallas_call x1, Pallas kernels: 20.5 us -> 19.4 us  [shards(): pl.pallas_call(functools.partial(kernel, nma, nf), out_shape=[field] * 2,...]
where the time goes in v3:
time: 20.9 us; the launch traced here: 20.8 us
  Pallas kernels  20.1 us (96%)
  between operations  0.64 us (3%)
    pallas_call x1, Pallas kernels, shards(): pl.pallas_call(functools.partial(kernel, nma, nf), out_shape=[field] * 2,...  19.4 us
    pallas_call x1, Pallas kernels, shards(): pl.pallas_call(write_out, out_shape=[jax.ShapeDtypeStruct(right_side.shap...  0.72 us

profile of v3, /device:TPU:0, one launch (start us, length us, event | category | flops | bytes accessed | tf_op | source)
XLA Modules:
  0.0 20.8 jit_solution(9539311938214763001)
XLA Ops:
  0.6 19.4 %solve.1 = (f32[8,4,2,512]{3,2,1,0:T(2,128)S(1)}, f32[8,4,2,512]{3,2,1,0:T(2,128)S(1)}) custom-call(f32[8,4,2,512]{3,2,1,0:T(2,128)} %rhs_in.1, f32[8,4,2,512]{3,2,1,0:T(2,128)} %x0_in.1, f32[8,4,2,16,512]{4,3,2,1,0:T(8,128)} %beam_in.1, f32[8,4,16]{2,1,0:T(4,128)} %noise_in.1, f32[1,512]{1,0:T(1,128)} %bitcast.2, f32[1,512]{1,0:T(1,128)} %bitcast.3), custom_call_target="tpu_custom_call" | custom-call | tf_op jit(solution)/shard_map/solve/pallas_call | solution.py:341
  20.1 0.7 %write_out.1 = (f32[8,4,2,512]{3,2,1,0:T(2,128)}, f32[8,4,2,512]{3,2,1,0:T(2,128)}) custom-call(f32[8,4,2,512]{3,2,1,0:T(2,128)S(1)} %get-tuple-element.4.sol_in, f32[8,4,2,512]{3,2,1,0:T(2,128)S(1)} %get-tuple-element.5.res_in), custom_call_target="tpu_custom_call" | custom-call | tf_op jit(solution)/shard_map/write_out/pallas_call | solution.py:370
